TPU v7x, 32 devices: a whole 2x2x4 slice. The times are simulated.
32 devices in a mesh: section: 4 (over y, x), dp: 2 (over core), mp: 4 (over z).
Axes of the slice: x: 2, y: 2, z: 4, core: 2. Of those that a mesh axis runs over, the one named last changes fastest.
Arguments:
- act_sent: bfloat16 [4, 16, 3072], P('section', ('dp', 'mp')), may hold values from -6 to 6
- new_batch: bfloat16 [16, 3072], P(('dp', 'mp')), may hold values from -6 to 6
- saved_input: bfloat16 [4, 16, 3072], P('section', ('dp', 'mp')), may hold values from -6 to 6
- grad_sent: bfloat16 [4, 16, 3072], P('section', ('dp', 'mp')), may hold values from -6 to 6
- loss_grad: bfloat16 [16, 3072], P(('dp', 'mp')), may hold values from -6 to 6
- ln_gain: float32 [4, 3072], P('section'), may hold values from 0.1 to 1.9
- w_in: bfloat16 [4, 3072, 16384], P('section', None, 'mp'), may hold values from -0.109375 to 0.109375
- w_out: bfloat16 [4, 3072, 16384], P('section', None, 'mp'), may hold values from -0.046875 to 0.046875
Outputs:
- act_out: bfloat16 [4, 16, 3072], P('section', ('dp', 'mp'))
- grad_out: bfloat16 [4, 16, 3072], P('section', ('dp', 'mp'))
- grad_w_in: bfloat16 [4, 3072, 16384], P('section', 'dp', 'mp')
- grad_w_out: bfloat16 [4, 3072, 16384], P('section', 'dp', 'mp')
All inputs are finite; a program needn't handle non-finite values.
Results may differ from a plain program's by a relative error of at most 0.0075.
Values may be sent and summed in bfloat16 or wider, within the bound.
No kernel may reach another device: no remote copies, remote signals or barrier semaphores. Data moves between devices by JAX's collectives and lax.ppermute only.
A program may use at most 128 MiB of HBM per device.

v0:
```python
import jax
import jax.numpy as jnp
from jax import lax
from jax.sharding import PartitionSpec as P

gelu_c = 0.7978845608028654


def from_behind(block, axis, distance):
    devices = range(lax.axis_size(axis))
    route = [(i - distance, i) for i in devices if i - distance in devices]
    return lax.ppermute(block, axis, route)


def gelu_pair(h):
    inner = gelu_c * (h + 0.044715 * h * h * h)
    tval = jnp.tanh(inner)
    value = 0.5 * h * (1.0 + tval)
    slope = 0.5 * (1.0 + tval) + 0.5 * h * (1.0 - tval * tval) * gelu_c * (
        1.0 + 3.0 * 0.044715 * h * h
    )
    return (value, slope)


def normalize(rows):
    xval = rows.astype(jnp.float32)
    centre = xval - jnp.mean(xval, axis=-1, keepdims=True)
    rstd = lax.rsqrt(jnp.mean(centre * centre, axis=-1, keepdims=True) + 1e-05)
    return (centre * rstd, rstd)


def contract_rows(left, right):
    return lax.dot_general(
        left, right, (((0,), (0,)), ((), ())), preferred_element_type=jnp.float32
    )


def per_device(act_sent, new_batch, saved_input, grad_sent, loss_grad, ln_gain, w_in, w_out):
    section_idx = lax.axis_index("section")
    sections = lax.axis_size("section")
    arrived = from_behind(act_sent, "section", 1)
    returned = from_behind(grad_sent, "section", -1)
    x_fwd = jnp.where(section_idx == 0, new_batch, arrived[0])
    upstream = jnp.where(section_idx == sections - 1, loss_grad, returned[0])
    gain = ln_gain[0]
    nhat_fwd, _ = normalize(x_fwd)
    n_fwd = (nhat_fwd * gain).astype(jnp.bfloat16)
    nhat_bwd, rstd_bwd = normalize(saved_input[0])
    n_bwd = (nhat_bwd * gain).astype(jnp.bfloat16)
    rows_fwd, rows_bwd, rows_up = (
        lax.all_gather(n_fwd, "mp", axis=0, tiled=True),
        lax.all_gather(n_bwd, "mp", axis=0, tiled=True),
        lax.all_gather(upstream, "mp", axis=0, tiled=True),
    )
    weight_in = w_in[0]
    weight_out = w_out[0]
    h_fwd = jnp.dot(rows_fwd, weight_in, preferred_element_type=jnp.float32)
    g_fwd = gelu_pair(h_fwd)[0].astype(jnp.bfloat16)
    branch_part = lax.dot_general(
        g_fwd, weight_out, (((1,), (1,)), ((), ())), preferred_element_type=jnp.float32
    )
    h_bwd = jnp.dot(rows_bwd, weight_in, preferred_element_type=jnp.float32)
    g_val, slope = gelu_pair(h_bwd)
    g_bwd = g_val.astype(jnp.bfloat16)
    grad_act = jnp.dot(rows_up, weight_out, preferred_element_type=jnp.float32)
    grad_hidden = (grad_act * slope).astype(jnp.bfloat16)
    norm_part = lax.dot_general(
        grad_hidden, weight_in, (((1,), (1,)), ((), ())), preferred_element_type=jnp.float32
    )
    branch_sum, grad_norm = (
        lax.psum_scatter(branch_part, "mp", scatter_dimension=0, tiled=True),
        lax.psum_scatter(norm_part, "mp", scatter_dimension=0, tiled=True),
    )
    act_out = (x_fwd.astype(jnp.float32) + branch_sum).astype(jnp.bfloat16)
    scaled = grad_norm * gain
    grad_in = upstream.astype(jnp.float32) + rstd_bwd * (
        scaled
        - jnp.mean(scaled, axis=-1, keepdims=True)
        - nhat_bwd * jnp.mean(scaled * nhat_bwd, axis=-1, keepdims=True)
    )
    all_norm, all_up, all_act, all_hidden = (
        lax.all_gather(rows_bwd, "dp", axis=0, tiled=True),
        lax.all_gather(rows_up, "dp", axis=0, tiled=True),
        lax.all_gather(g_bwd, "dp", axis=0, tiled=True),
        lax.all_gather(grad_hidden, "dp", axis=0, tiled=True),
    )
    replicas = lax.axis_size("dp")
    half = weight_in.shape[0] // replicas
    start = lax.axis_index("dp") * half
    cols_norm = lax.dynamic_slice_in_dim(all_norm, start, half, 1)
    cols_up = lax.dynamic_slice_in_dim(all_up, start, half, 1)
    block = rows_bwd.shape[0]
    sum_in = jnp.zeros((half, weight_in.shape[1]), jnp.float32)
    sum_out = jnp.zeros((half, weight_in.shape[1]), jnp.float32)
    for replica in range(replicas):
        low = replica * block
        term_in = contract_rows(cols_norm[low : low + block], all_hidden[low : low + block])
        term_out = contract_rows(cols_up[low : low + block], all_act[low : low + block])
        sum_in = sum_in + term_in.astype(jnp.bfloat16).astype(jnp.float32)
        sum_out = sum_out + term_out.astype(jnp.bfloat16).astype(jnp.float32)
    return (
        act_out[None],
        grad_in.astype(jnp.bfloat16)[None],
        sum_in.astype(jnp.bfloat16)[None],
        sum_out.astype(jnp.bfloat16)[None],
    )


def solution(mesh):
    return jax.shard_map(
        per_device,
        mesh=mesh,
        in_specs=(
            P("section", ("dp", "mp"), None),
            P(("dp", "mp"), None),
            P("section", ("dp", "mp"), None),
            P("section", ("dp", "mp"), None),
            P(("dp", "mp"), None),
            P("section", None),
            P("section", None, "mp"),
            P("section", None, "mp"),
        ),
        out_specs=(
            P("section", ("dp", "mp"), None),
            P("section", ("dp", "mp"), None),
            P("section", "dp", "mp"),
            P("section", "dp", "mp"),
        ),
        check_vma=False,
    )
```

profile of v0, /device:TPU:0, one launch (start us, length us, event | category | flops | bytes accessed | tf_op | source)
XLA Modules:
  0.0 181.2 jit_solution(3140549871322711195)
XLA Ops:
  7.2 0.0 all-reduce.5.cloned.1.call-start
  7.2 4.9 %collective-permute-start = (bf16[1,2,3072]{2,1,0:T(2,128)(2,1)}, bf16[1,2,3072]{2,1,0:T(2,128)(2,1)S(1)}, u32[]{:S(2)}, u32[]{:S(2)}) collective-permute-start(bf16[1,2,3072]{2,1,0:T(2,128)(2,1)} %param.8), channel_id=1, source_target_pairs={{0,8},{8,16},{16,24},{1,9},{9,17},{17,25},{2,10},{10,18},{18,26},{... | collective-permute-start | bytes 36872 | tf_op jit(solution)/shard_map/ppermute | solution.py:12
  12.1 1.3 collective-permute-start.1
  13.4 0.8 convert_reduce_fusion.1
  14.2 0.9 fusion.48
  15.2 1.2 dynamic-slice
  17.1 0.0 collective-permute-done
  17.1 0.9 convert_reduce_fusion
  17.9 0.2 fusion.42
  18.2 0.8 fusion.55
  19.0 13.4 %all-gather.2 = bf16[4,2,3072]{2,1,0:T(2,128)(2,1)S(1)} all-gather(bf16[1,2,3072]{2,1,0:T(2,128)(2,1)S(1)} %get-tuple-element.10), channel_id=1, replica_groups=mesh['section'=4,'dp'=2,'mp'=4] {'mp'}, dimensions={0}, use_global_device_ids=true | all-gather | bytes 61440 | tf_op jit(solution)/shard_map/all_gather | solution.py:52
  32.4 0.0 collective-permute-done.1
  32.4 13.1 %all-gather.1 = bf16[4,2,3072]{2,1,0:T(2,128)(2,1)S(1)} all-gather(bf16[1,2,3072]{2,1,0:T(2,128)(2,1)S(1)} %fusion.60), channel_id=1, replica_groups=mesh['section'=4,'dp'=2,'mp'=4] {'mp'}, dimensions={0}, use_global_device_ids=true | all-gather | bytes 61440 | tf_op jit(solution)/shard_map/all_gather | solution.py:53
  45.6 1.9 %all_gather.26 = bf16[16,3072]{1,0:T(8,128)(2,1)S(1)} all-gather(bf16[8,3072]{1,0:T(8,128)(2,1)S(1)} %reshape.44), channel_id=1, replica_groups=mesh['section'=4,'dp'=2,'mp'=4] {'dp'}, dimensions={0}, use_global_device_ids=true | all-gather | bytes 147456 | tf_op jit(solution)/shard_map/all_gather | solution.py:83
  47.4 1.9 %all_gather.24 = bf16[16,3072]{1,0:T(8,128)(2,1)S(1)} all-gather(bf16[8,3072]{1,0:T(8,128)(2,1)S(1)} %reshape.46), channel_id=1, replica_groups=mesh['section'=4,'dp'=2,'mp'=4] {'dp'}, dimensions={0}, use_global_device_ids=true | all-gather | bytes 147456 | tf_op jit(solution)/shard_map/all_gather | solution.py:82
  49.3 9.9 %multiply_convert_fusion = (bf16[8,4096]{1,0:T(8,128)(2,1)S(1)}, f32[8,4096]{1,0:T(8,128)S(1)}) fusion(bf16[8,3072]{1,0:T(8,128)(2,1)S(1)} %reshape.46, bf16[1,3072,4096]{2,1,0:T(8,128)(2,1)} %param.14), kind=kOutput, calls=%fused_computation.33 | convolution fusion | flops 201621504 | bytes 25411584 | tf_op jit(solution)/shard_map/dot_general | solution.py:62
  59.2 10.0 %fusion.15 = bf16[8,4096]{1,0:T(8,128)(2,1)S(1)} fusion(bf16[8,3072]{1,0:T(8,128)(2,1)S(1)} %reshape.44, bf16[1,3072,4096]{2,1,0:T(8,128)(2,1)} %param.15, f32[8,4096]{1,0:T(8,128)S(1)} %get-tuple-element.13), kind=kOutput, calls=%fused_computation.19 | convolution fusion | flops 201949184 | bytes 25411584 | tf_op jit(solution)/shard_map/dot_general | solution.py:65
  69.2 12.2 %fusion.4 = f32[8,3072]{1,0:T(8,128)} fusion(bf16[8,4096]{1,0:T(8,128)(2,1)S(1)} %fusion.15, bf16[1,3072,4096]{2,1,0:T(8,128)(2,1)} %param.14), kind=kOutput, calls=%fused_computation.4 | convolution fusion | flops 201326592 | bytes 25329664 | tf_op jit(solution)/shard_map/dot_general | solution.py:67
  81.4 1.9 %all_gather.25 = bf16[16,4096]{1,0:T(8,128)(2,1)S(1)} all-gather(bf16[8,4096]{1,0:T(8,128)(2,1)S(1)} %fusion.15), channel_id=1, replica_groups=mesh['section'=4,'dp'=2,'mp'=4] {'dp'}, dimensions={0}, use_global_device_ids=true | all-gather | bytes 196608 | tf_op jit(solution)/shard_map/all_gather | solution.py:85
  83.3 13.1 %all-gather = bf16[4,2,3072]{2,1,0:T(2,128)(2,1)S(1)} all-gather(bf16[1,2,3072]{2,1,0:T(2,128)(2,1)S(1)} %get-tuple-element.11), channel_id=1, replica_groups=mesh['section'=4,'dp'=2,'mp'=4] {'mp'}, dimensions={0}, use_global_device_ids=true | all-gather | bytes 61440 | tf_op jit(solution)/shard_map/all_gather | solution.py:51
  96.4 19.8 %fusion.2 = f32[8,3072]{1,0:T(8,128)} fusion(bf16[1,3072,4096]{2,1,0:T(8,128)(2,1)} %param.15, bf16[8,3072]{1,0:T(8,128)(2,1)S(1)} %reshape.42, bf16[1,3072,4096]{2,1,0:T(8,128)(2,1)} %param.14), kind=kOutput, calls=%fused_computation.2 | convolution fusion | flops 402948096 | bytes 50479104 | tf_op jit(solution)/shard_map/dot_general | solution.py:59
  116.1 2.1 %all_gather.27 = bf16[16,4096]{1,0:T(8,128)(2,1)S(1)} all-gather(bf16[8,4096]{1,0:T(8,128)(2,1)S(1)} %get-tuple-element.12), channel_id=1, replica_groups=mesh['section'=4,'dp'=2,'mp'=4] {'dp'}, dimensions={0}, use_global_device_ids=true | all-gather | bytes 196608 | tf_op jit(solution)/shard_map/all_gather | solution.py:84
  118.2 6.6 %convolution_convert_fusion.2 = bf16[1536,4096]{1,0:T(8,128)(2,1)} fusion(bf16[16,4096]{1,0:T(8,128)(2,1)S(1)} %all_gather.25, bf16[16,3072]{1,0:T(8,128)(2,1)S(1)} %all_gather.24, s32[]{:T(128)S(6)} %add.72, s32[]{:T(128)S(6)} %select_n.22), kind=kOutput, calls=%fused_computation.14 | convolution fusion | flops 106954752 | bytes 12673032 | tf_op jit(solution)/shard_map/dot_general | solution.py:33
  124.8 9.4 %fusion.10 = bf16[1,1536,4096]{2,1,0:T(8,128)(2,1)} fusion(bf16[1536,4096]{1,0:T(8,128)(2,1)} %convolution_convert_fusion.2, bf16[16,4096]{1,0:T(8,128)(2,1)S(1)} %all_gather.25, bf16[16,3072]{1,0:T(8,128)(2,1)S(1)} %all_gather.24, s32[]{:T(128)S(6)} %select_n.22), kind=kOutput, calls=%fused_computation.16 | convolution fusion | flops 132120576 | bytes 25255940 | tf_op jit(solution)/shard_map/dot_general | solution.py:33
  134.2 0.0 all-reduce.5.cloned.1.call-update
  134.2 0.0 copy-start
  134.2 0.0 copy-start.1
  134.3 0.0 copy-start.2
  134.3 6.6 %convolution_convert_fusion = bf16[1536,4096]{1,0:T(8,128)(2,1)} fusion(bf16[16,4096]{1,0:T(8,128)(2,1)S(1)} %all_gather.27, bf16[16,3072]{1,0:T(8,128)(2,1)S(1)} %all_gather.26, s32[]{:T(128)S(6)} %add.72, s32[]{:T(128)S(6)} %select_n.22), kind=kOutput, calls=%fused_computation.12 | convolution fusion | flops 106954752 | bytes 12673032 | tf_op jit(solution)/shard_map/dot_general | solution.py:33
  140.9 9.4 %fusion.11 = bf16[1,1536,4096]{2,1,0:T(8,128)(2,1)} fusion(bf16[1536,4096]{1,0:T(8,128)(2,1)} %convolution_convert_fusion, bf16[16,4096]{1,0:T(8,128)(2,1)S(1)} %all_gather.27, bf16[16,3072]{1,0:T(8,128)(2,1)S(1)} %all_gather.26, s32[]{:T(128)S(6)} %select_n.22), kind=kOutput, calls=%fused_computation.17 | convolution fusion | flops 132120576 | bytes 25255940 | tf_op jit(solution)/shard_map/dot_general | solution.py:33
  150.3 21.2 %all-reduce.5.cloned.1.call-done = (f32[8,3072]{1,0:T(8,128)}, f32[8,3072]{1,0:T(8,128)}) async-done(((f32[8,3072]{1,0:T(8,128)}, f32[8,3072]{1,0:T(8,128)}), (f32[8,3072]{1,0:T(8,128)}, f32[8,3072]{1,0:T(8,128)})) %all-reduce.5.cloned.1.call-update) | async-done | bytes 196624
  171.5 0.0 copy-done
  171.6 0.0 copy-done.1
  171.6 1.1 fusion.65
  172.7 0.0 copy-done.2
  172.7 1.7 fusion.54
  (10 shorter events, 0.1 us)
Async XLA Ops:
  7.2 164.4 %all-reduce.5.cloned.1.call-start = ((), (), s32[]{:S(2)}) async-start(), calls=%async_computation | async-start | bytes 393216
  7.2 9.9 %collective-permute-start = (bf16[1,2,3072]{2,1,0:T(2,128)(2,1)}, bf16[1,2,3072]{2,1,0:T(2,128)(2,1)S(1)}, u32[]{:S(2)}, u32[]{:S(2)}) collective-permute-start(bf16[1,2,3072]{2,1,0:T(2,128)(2,1)} %param.8), channel_id=1, source_target_pairs={{0,8},{8,16},{16,24},{1,9},{9,17},{17,25},{2,10},{10,18},{18,26},{... | collective-permute-start | bytes 36872 | tf_op jit(solution)/shard_map/ppermute | solution.py:12
  12.1 20.3 %collective-permute-start.1 = (bf16[1,2,3072]{2,1,0:T(2,128)(2,1)}, bf16[1,2,3072]{2,1,0:T(2,128)(2,1)S(1)}, u32[]{:S(2)}, u32[]{:S(2)}) collective-permute-start(bf16[1,2,3072]{2,1,0:T(2,128)(2,1)} %param.11), channel_id=1, source_target_pairs={{8,0},{16,8},{24,16},{9,1},{17,9},{25,17},{10,2},{18,10},{26,18},{... | collective-permute-start | bytes 36872 | tf_op jit(solution)/shard_map/ppermute | solution.py:12
  134.2 37.3 %copy-start = (bf16[1,2,3072]{2,1,0:T(2,128)(2,1)S(1)}, bf16[1,2,3072]{2,1,0:T(2,128)(2,1)}, u32[]{:S(2)}) copy-start(bf16[1,2,3072]{2,1,0:T(2,128)(2,1)} %param.10) | copy-start | bytes 36868
  134.2 37.3 %copy-start.1 = (f32[1,3072]{1,0:T(1,128)S(1)}, f32[1,3072]{1,0:T(1,128)}, u32[]{:S(2)}) copy-start(f32[1,3072]{1,0:T(1,128)} %param.13) | copy-start | bytes 36868
  134.3 38.4 %copy-start.2 = (bf16[2,3072]{1,0:T(2,128)(2,1)S(1)}, bf16[2,3072]{1,0:T(2,128)(2,1)}, u32[]{:S(2)}) copy-start(bf16[2,3072]{1,0:T(2,128)(2,1)} %param.12) | copy-start | bytes 36868
Sparse Core Ops, SparseCore 0:
  134.4 37.1 all-reduce.4
where the time goes:
time: 182 us; the launch traced here: 181 us
  matrix products  83.9 us (46%)
  blocking collectives  47.2 us (26%)
  waiting for transfers between devices  21.2 us (12%)
  between operations  14.8 us (8%)
  other arithmetic  6.5 us (4%)
  starting transfers between devices  6.2 us (3%)
    dot_general x4, matrix products, contract_rows(): lax.dot_general(left, right, (((0,), (0,)), ((), ())), preferred_element_...  32.1 us
    unnamed x2, waiting for transfers between devices  21.2 us
    dot_general x1, matrix products, per_device(): lax.dot_general(g_fwd, weight_out, (((1,), (1,)), ((), ())), preferred_el...  19.8 us
    all_gather x1, blocking collectives, per_device(): lax.all_gather(n_bwd, 'mp', axis=0, tiled=True)  13.4 us
    all_gather x1, blocking collectives, per_device(): lax.all_gather(upstream, 'mp', axis=0, tiled=True)  13.1 us
    all_gather x1, blocking collectives, per_device(): lax.all_gather(n_fwd, 'mp', axis=0, tiled=True)  13.1 us
    dot_general x1, matrix products, per_device(): lax.dot_general(grad_hidden, weight_in, (((1,), (1,)), ((), ())), preferr...  12.2 us
    dot_general x1, matrix products, per_device(): grad_act = jnp.dot(rows_up, weight_out, preferred_element_type=jnp.float32)  10 us
  transfers between devices with their start and end apart: 3, of which 1 were waited for; matrix products, arithmetic and copies ran while one was open for 12% of the time, Pallas kernels for 0%

commit v1 on v0

--- a/solution.py
+++ b/solution.py
@@ -2,8 +2,34 @@
 import jax.numpy as jnp
 from jax import lax
 from jax.sharding import PartitionSpec as P
+from jax.lax import axis_index, axis_size, ppermute
 
 gelu_c = 0.7978845608028654
+
+
+def _pack_node(point):
+    mesh_ax = "mp"
+    left_arr = axis_size(mesh_ax)
+    shaped = axis_index(mesh_ax)
+    m_next, z_new, arr_out = (left_arr, shaped, point.shape[0])
+    part_next = lax.dynamic_update_slice_in_dim(
+        jnp.zeros(
+            [ix * m_next if i0 == 0 else ix for i0, ix in enumerate(point.shape)], point.dtype
+        ),
+        point,
+        z_new * arr_out,
+        axis=0,
+    )
+    for pp in range(1, m_next):
+        point = ppermute(
+            point,
+            axis_name=mesh_ax,
+            perm=list(map(lambda i0: (i0, (i0 + 1) % m_next), range(m_next))),
+        )
+        part_next = lax.dynamic_update_slice_in_dim(
+            part_next, point, (z_new - pp) % m_next * arr_out, axis=0
+        )
+    return part_next
 
 
 def from_behind(block, axis, distance):
@@ -49,7 +75,7 @@
     n_bwd = (nhat_bwd * gain).astype(jnp.bfloat16)
     rows_fwd, rows_bwd, rows_up = (
         lax.all_gather(n_fwd, "mp", axis=0, tiled=True),
-        lax.all_gather(n_bwd, "mp", axis=0, tiled=True),
+        _pack_node(n_bwd),
         lax.all_gather(upstream, "mp", axis=0, tiled=True),
     )
     weight_in = w_in[0]

time: 182 us -> 161 us (0.88)
  blocking collectives: 47.2 us -> 34.1 us
  waiting for transfers between devices: 21.2 us -> 10.8 us
  starting transfers between devices: 6.2 us -> 8.17 us
    unnamed x2, waiting for transfers between devices: 21.2 us -> 2.03 us
    all_gather x1 -> x0, blocking collectives: 13.4 us -> none  [per_device(): lax.all_gather(n_bwd, 'mp', axis=0, tiled=True)]
    ppermute x0 -> x3, waiting for transfers between devices: none -> 8.77 us  [_pack_node(): ppermute(point, axis_name=mesh_ax, perm=list(map(lambda i0: (i0, (i0 + 1)...]
    ppermute x0 -> x3, starting transfers between devices: none -> 1.97 us  [_pack_node(): ppermute(point, axis_name=mesh_ax, perm=list(map(lambda i0: (i0, (i0 + 1)...]
  transfers between devices with their start and end apart: 3 -> 6, of which waited for: 1 -> 3; matrix products, arithmetic and copies ran while one was open for 12% -> 36% of each run, Pallas kernels for 0% -> 0%
where the time goes in v1:
time: 161 us; the launch traced here: 160 us
  matrix products  83.9 us (52%)
  blocking collectives  34.1 us (21%)
  between operations  14.8 us (9%)
  waiting for transfers between devices  10.8 us (7%)
  starting transfers between devices  8.17 us (5%)
  other arithmetic  7.29 us (5%)
    dot_general x4, matrix products, contract_rows(): lax.dot_general(left, right, (((0,), (0,)), ((), ())), preferred_element_...  32 us
    dot_general x1, matrix products, per_device(): lax.dot_general(g_fwd, weight_out, (((1,), (1,)), ((), ())), preferred_el...  19.8 us
    all_gather x1, blocking collectives, per_device(): lax.all_gather(n_fwd, 'mp', axis=0, tiled=True)  13.3 us
    all_gather x1, blocking collectives, per_device(): lax.all_gather(upstream, 'mp', axis=0, tiled=True)  13.1 us
    dot_general x1, matrix products, per_device(): lax.dot_general(grad_hidden, weight_in, (((1,), (1,)), ((), ())), preferr...  12.2 us
    dot_general x1, matrix products, per_device(): grad_act = jnp.dot(rows_up, weight_out, preferred_element_type=jnp.float32)  10 us
    dot_general x1, matrix products, per_device(): h_bwd = jnp.dot(rows_bwd, weight_in, preferred_element_type=jnp.float32)  9.92 us
    ppermute x3, waiting for transfers between devices, _pack_node(): ppermute(point, axis_name=mesh_ax, perm=list(map(lambda i0: (i0, (i0 + 1)...  8.77 us
  transfers between devices with their start and end apart: 6, of which 3 were waited for; matrix products, arithmetic and copies ran while one was open for 36% of the time, Pallas kernels for 0%

profile of v1, /device:TPU:0, one launch (start us, length us, event | category | flops | bytes accessed | tf_op | source)
XLA Modules:
  0.0 160.4 jit_solution(3223563384224370090)
XLA Ops:
  7.2 0.0 all-reduce.5.cloned.1.call-start
  7.2 4.9 %collective-permute-start = (bf16[1,2,3072]{2,1,0:T(2,128)(2,1)}, bf16[1,2,3072]{2,1,0:T(2,128)(2,1)S(1)}, u32[]{:S(2)}, u32[]{:S(2)}) collective-permute-start(bf16[1,2,3072]{2,1,0:T(2,128)(2,1)} %param.8), channel_id=1, source_target_pairs={{0,8},{8,16},{16,24},{1,9},{9,17},{17,25},{2,10},{10,18},{18,26},{... | collective-permute-start | bytes 36872 | tf_op jit(solution)/shard_map/ppermute | solution.py:38
  12.1 1.3 collective-permute-start.1
  13.4 0.8 convert_reduce_fusion.1
  14.2 0.9 fusion.48
  15.2 0.8 constant_dynamic-update-slice_fusion.3
  16.0 1.6 %collective-permute-start.2 = (bf16[2,3072]{1,0:T(2,128)(2,1)S(1)}, bf16[2,3072]{1,0:T(2,128)(2,1)S(1)}, u32[]{:S(2)}, u32[]{:S(2)}) collective-permute-start(bf16[2,3072]{1,0:T(2,128)(2,1)S(1)} %get-tuple-element.9), channel_id=1, source_target_pairs={{0,1},{1,2},{2,3},{3,0},{4,5},{5,6},{6,7},{7,4},{8,9},{9,10},{10,1... | collective-permute-start | bytes 36872 | tf_op jit(solution)/shard_map/ppermute | solution.py:24
  17.6 1.2 dynamic-slice
  19.5 0.0 collective-permute-done
  19.5 0.9 convert_reduce_fusion
  20.4 0.2 fusion.42
  20.6 0.8 fusion.55
  21.4 13.3 %all-gather = bf16[4,2,3072]{2,1,0:T(2,128)(2,1)S(1)} all-gather(bf16[1,2,3072]{2,1,0:T(2,128)(2,1)S(1)} %fusion.55), channel_id=1, replica_groups=mesh['section'=4,'dp'=2,'mp'=4] {'mp'}, dimensions={0}, use_global_device_ids=true | all-gather | bytes 61440 | tf_op jit(solution)/shard_map/all_gather | solution.py:77
  34.7 0.0 copy-start.2
  34.8 19.8 %fusion.2 = f32[8,3072]{1,0:T(8,128)} fusion(bf16[1,3072,4096]{2,1,0:T(8,128)(2,1)} %param.15, bf16[8,3072]{1,0:T(8,128)(2,1)S(1)} %reshape.42, bf16[1,3072,4096]{2,1,0:T(8,128)(2,1)} %param.14), kind=kOutput, calls=%fused_computation.2 | convolution fusion | flops 402948096 | bytes 50479104 | tf_op jit(solution)/shard_map/dot_general | solution.py:85
  54.5 0.0 collective-permute-done.1
  54.5 0.0 copy-done.2
  54.5 13.1 %all-gather.1 = bf16[4,2,3072]{2,1,0:T(2,128)(2,1)S(1)} all-gather(bf16[1,2,3072]{2,1,0:T(2,128)(2,1)S(1)} %fusion.59), channel_id=1, replica_groups=mesh['section'=4,'dp'=2,'mp'=4] {'mp'}, dimensions={0}, use_global_device_ids=true | all-gather | bytes 61440 | tf_op jit(solution)/shard_map/all_gather | solution.py:79
  67.6 0.0 collective-permute-done.2
  67.7 0.3 collective-permute-start.3
  68.0 1.9 %all_gather.22 = bf16[16,3072]{1,0:T(8,128)(2,1)S(1)} all-gather(bf16[8,3072]{1,0:T(8,128)(2,1)S(1)} %reshape.44), channel_id=1, replica_groups=mesh['section'=4,'dp'=2,'mp'=4] {'dp'}, dimensions={0}, use_global_device_ids=true | all-gather | bytes 147456 | tf_op jit(solution)/shard_map/all_gather | solution.py:109
  69.9 3.3 %collective-permute-done.3 = bf16[2,3072]{1,0:T(2,128)(2,1)S(1)} collective-permute-done((bf16[2,3072]{1,0:T(2,128)(2,1)S(1)}, bf16[2,3072]{1,0:T(2,128)(2,1)S(1)}, u32[]{:S(2)}, u32[]{:S(2)}) %collective-permute-start.3) | collective-permute-done | bytes 12320 | tf_op jit(solution)/shard_map/ppermute | solution.py:24
  73.2 0.0 collective-permute-start.4
  73.2 5.5 %collective-permute-done.4 = bf16[2,3072]{1,0:T(2,128)(2,1)S(1)} collective-permute-done((bf16[2,3072]{1,0:T(2,128)(2,1)S(1)}, bf16[2,3072]{1,0:T(2,128)(2,1)S(1)}, u32[]{:S(2)}, u32[]{:S(2)}) %collective-permute-start.4) | collective-permute-done | bytes 12320 | tf_op jit(solution)/shard_map/ppermute | solution.py:24
  78.7 1.9 %all_gather.20 = bf16[16,3072]{1,0:T(8,128)(2,1)S(1)} all-gather(bf16[8,3072]{1,0:T(8,128)(2,1)S(1)} %constant_dynamic-update-slice_fusion), channel_id=1, replica_groups=mesh['section'=4,'dp'=2,'mp'=4] {'dp'}, dimensions={0}, use_global_device_ids=true | all-gather | bytes 147456 | tf_op jit(solution)/shard_map/all_gather | solution.py:108
  80.6 9.9 %multiply_convert_fusion = (bf16[8,4096]{1,0:T(8,128)(2,1)S(1)}, f32[8,4096]{1,0:T(8,128)S(1)}) fusion(bf16[8,3072]{1,0:T(8,128)(2,1)S(1)} %constant_dynamic-update-slice_fusion, bf16[1,3072,4096]{2,1,0:T(8,128)(2,1)} %param.14), kind=kOutput, calls=%fused_computation.33 | convolution fusion | flops 201621504 | bytes 25411584 | tf_op jit(solution)/shard_map/dot_general | solution.py:88
  90.5 10.0 %fusion.15 = bf16[8,4096]{1,0:T(8,128)(2,1)S(1)} fusion(bf16[8,3072]{1,0:T(8,128)(2,1)S(1)} %reshape.44, bf16[1,3072,4096]{2,1,0:T(8,128)(2,1)} %param.15, f32[8,4096]{1,0:T(8,128)S(1)} %get-tuple-element.13), kind=kOutput, calls=%fused_computation.19 | convolution fusion | flops 201949184 | bytes 25411584 | tf_op jit(solution)/shard_map/dot_general | solution.py:91
  100.5 12.2 %fusion.4 = f32[8,3072]{1,0:T(8,128)} fusion(bf16[8,4096]{1,0:T(8,128)(2,1)S(1)} %fusion.15, bf16[1,3072,4096]{2,1,0:T(8,128)(2,1)} %param.14), kind=kOutput, calls=%fused_computation.4 | convolution fusion | flops 201326592 | bytes 25329664 | tf_op jit(solution)/shard_map/dot_general | solution.py:93
  112.7 1.9 %all_gather.21 = bf16[16,4096]{1,0:T(8,128)(2,1)S(1)} all-gather(bf16[8,4096]{1,0:T(8,128)(2,1)S(1)} %fusion.15), channel_id=1, replica_groups=mesh['section'=4,'dp'=2,'mp'=4] {'dp'}, dimensions={0}, use_global_device_ids=true | all-gather | bytes 196608 | tf_op jit(solution)/shard_map/all_gather | solution.py:111
  114.6 2.1 %all_gather.23 = bf16[16,4096]{1,0:T(8,128)(2,1)S(1)} all-gather(bf16[8,4096]{1,0:T(8,128)(2,1)S(1)} %get-tuple-element.12), channel_id=1, replica_groups=mesh['section'=4,'dp'=2,'mp'=4] {'dp'}, dimensions={0}, use_global_device_ids=true | all-gather | bytes 196608 | tf_op jit(solution)/shard_map/all_gather | solution.py:110
  116.7 0.0 all-reduce.5.cloned.1.call-update
  116.7 6.6 %convolution_convert_fusion.3 = bf16[1536,4096]{1,0:T(8,128)(2,1)} fusion(bf16[16,4096]{1,0:T(8,128)(2,1)S(1)} %all_gather.21, bf16[16,3072]{1,0:T(8,128)(2,1)S(1)} %all_gather.20, s32[]{:T(128)S(6)} %select_n.56), kind=kOutput, calls=%fused_computation.15 | convolution fusion | flops 106954752 | bytes 12673028 | tf_op jit(solution)/shard_map/dot_general | solution.py:59
  123.3 9.4 %fusion.10 = bf16[1,1536,4096]{2,1,0:T(8,128)(2,1)} fusion(bf16[1536,4096]{1,0:T(8,128)(2,1)} %convolution_convert_fusion.3, bf16[16,4096]{1,0:T(8,128)(2,1)S(1)} %all_gather.21, bf16[16,3072]{1,0:T(8,128)(2,1)S(1)} %all_gather.20, s32[]{:T(128)S(6)} %add.104, s32[]{:T(128)S(6)} %select_n.56), kind=kOutput, calls=%fused_computation.16 | convolution fusion | flops 132120576 | bytes 25255944 | tf_op jit(solution)/shard_map/dot_general | solution.py:59
  132.7 0.0 copy-start
  132.7 0.0 copy-start.1
  132.7 6.6 %convolution_convert_fusion = bf16[1536,4096]{1,0:T(8,128)(2,1)} fusion(bf16[16,4096]{1,0:T(8,128)(2,1)S(1)} %all_gather.23, bf16[16,3072]{1,0:T(8,128)(2,1)S(1)} %all_gather.22, s32[]{:T(128)S(6)} %add.104, s32[]{:T(128)S(6)} %select_n.56), kind=kOutput, calls=%fused_computation.12 | convolution fusion | flops 106954752 | bytes 12673032 | tf_op jit(solution)/shard_map/dot_general | solution.py:59
  139.3 9.4 %fusion.11 = bf16[1,1536,4096]{2,1,0:T(8,128)(2,1)} fusion(bf16[1536,4096]{1,0:T(8,128)(2,1)} %convolution_convert_fusion, bf16[16,4096]{1,0:T(8,128)(2,1)S(1)} %all_gather.23, bf16[16,3072]{1,0:T(8,128)(2,1)S(1)} %all_gather.22, s32[]{:T(128)S(6)} %select_n.56), kind=kOutput, calls=%fused_computation.17 | convolution fusion | flops 132120576 | bytes 25255940 | tf_op jit(solution)/shard_map/dot_general | solution.py:59
  148.7 2.0 %all-reduce.5.cloned.1.call-done = (f32[8,3072]{1,0:T(8,128)}, f32[8,3072]{1,0:T(8,128)}) async-done(((f32[8,3072]{1,0:T(8,128)}, f32[8,3072]{1,0:T(8,128)}), (f32[8,3072]{1,0:T(8,128)}, f32[8,3072]{1,0:T(8,128)})) %all-reduce.5.cloned.1.call-update) | async-done | bytes 196624
  150.7 0.0 copy-done
  150.7 0.0 copy-done.1
  150.7 1.1 fusion.64
  151.9 1.7 %fusion.54 = (bf16[1,2,3072]{2,1,0:T(2,128)(2,1)}, bf16[1,2,3072]{2,1,0:T(2,128)(2,1)}) fusion(f32[8,3072]{1,0:T(8,128)} %get-tuple-element.6, u32[]{:T(128)S(6)} %multiply.37, bf16[2,3072]{1,0:T(2,128)(2,1)S(1)} %get-tuple-element.11, f32[2]{0:T(128)S(1)} %broadcast_multiply_fusion, f32[2]{0:T(128)S(1)} %broadcast_multiply_fusion.2, ...), kind=kLoop, calls=%fused_computation.67 | loop fusion | flops 92160 | bytes 135205 | tf_op jit(solution)/shard_map/broadcast_in_dim | solution.py:128
  (13 shorter events, 0.2 us)
Async XLA Ops:
  7.2 143.6 %all-reduce.5.cloned.1.call-start = ((), (), s32[]{:S(2)}) async-start(), calls=%async_computation | async-start | bytes 393216
  7.2 12.3 %collective-permute-start = (bf16[1,2,3072]{2,1,0:T(2,128)(2,1)}, bf16[1,2,3072]{2,1,0:T(2,128)(2,1)S(1)}, u32[]{:S(2)}, u32[]{:S(2)}) collective-permute-start(bf16[1,2,3072]{2,1,0:T(2,128)(2,1)} %param.8), channel_id=1, source_target_pairs={{0,8},{8,16},{16,24},{1,9},{9,17},{17,25},{2,10},{10,18},{18,26},{... | collective-permute-start | bytes 36872 | tf_op jit(solution)/shard_map/ppermute | solution.py:38
  12.1 42.4 %collective-permute-start.1 = (bf16[1,2,3072]{2,1,0:T(2,128)(2,1)}, bf16[1,2,3072]{2,1,0:T(2,128)(2,1)S(1)}, u32[]{:S(2)}, u32[]{:S(2)}) collective-permute-start(bf16[1,2,3072]{2,1,0:T(2,128)(2,1)} %param.11), channel_id=1, source_target_pairs={{8,0},{16,8},{24,16},{9,1},{17,9},{25,17},{10,2},{18,10},{26,18},{... | collective-permute-start | bytes 36872 | tf_op jit(solution)/shard_map/ppermute | solution.py:38
  16.0 51.6 %collective-permute-start.2 = (bf16[2,3072]{1,0:T(2,128)(2,1)S(1)}, bf16[2,3072]{1,0:T(2,128)(2,1)S(1)}, u32[]{:S(2)}, u32[]{:S(2)}) collective-permute-start(bf16[2,3072]{1,0:T(2,128)(2,1)S(1)} %get-tuple-element.9), channel_id=1, source_target_pairs={{0,1},{1,2},{2,3},{3,0},{4,5},{5,6},{6,7},{7,4},{8,9},{9,10},{10,1... | collective-permute-start | bytes 36872 | tf_op jit(solution)/shard_map/ppermute | solution.py:24
  34.7 19.8 %copy-start.2 = (bf16[2,3072]{1,0:T(2,128)(2,1)S(1)}, bf16[2,3072]{1,0:T(2,128)(2,1)}, u32[]{:S(2)}) copy-start(bf16[2,3072]{1,0:T(2,128)(2,1)} %param.12) | copy-start | bytes 36868
  67.7 5.5 %collective-permute-start.3 = (bf16[2,3072]{1,0:T(2,128)(2,1)S(1)}, bf16[2,3072]{1,0:T(2,128)(2,1)S(1)}, u32[]{:S(2)}, u32[]{:S(2)}) collective-permute-start(bf16[2,3072]{1,0:T(2,128)(2,1)S(1)} %collective-permute-done.2), channel_id=1, source_target_pairs={{0,1},{1,2},{2,3},{3,0},{4,5},{5,6},{6,7},{7,4},{8,9},{9,10},{10,1... | collective-permute-start | bytes 36872 | tf_op jit(solution)/shard_map/ppermute | solution.py:24
  73.2 5.5 %collective-permute-start.4 = (bf16[2,3072]{1,0:T(2,128)(2,1)S(1)}, bf16[2,3072]{1,0:T(2,128)(2,1)S(1)}, u32[]{:S(2)}, u32[]{:S(2)}) collective-permute-start(bf16[2,3072]{1,0:T(2,128)(2,1)S(1)} %collective-permute-done.3), channel_id=1, source_target_pairs={{0,1},{1,2},{2,3},{3,0},{4,5},{5,6},{6,7},{7,4},{8,9},{9,10},{10,1... | collective-permute-start | bytes 36872 | tf_op jit(solution)/shard_map/ppermute | solution.py:24
  132.7 18.0 %copy-start = (bf16[1,2,3072]{2,1,0:T(2,128)(2,1)S(1)}, bf16[1,2,3072]{2,1,0:T(2,128)(2,1)}, u32[]{:S(2)}) copy-start(bf16[1,2,3072]{2,1,0:T(2,128)(2,1)} %param.10) | copy-start | bytes 36868
  132.7 18.0 %copy-start.1 = (f32[1,3072]{1,0:T(1,128)S(1)}, f32[1,3072]{1,0:T(1,128)}, u32[]{:S(2)}) copy-start(f32[1,3072]{1,0:T(1,128)} %param.13) | copy-start | bytes 36868
Sparse Core Ops, SparseCore 0:
  116.8 33.8 all-reduce.4
